TPU v7x, 32 devices: a whole 2x2x4 slice. The times are simulated.
32 devices in a mesh: seq: 4 (over y, x), ep: 8 (over z, core).
Axes of the slice: x: 2, y: 2, z: 4, core: 2. Of those that a mesh axis runs over, the one named last changes fastest.
Arguments:
- tokens: bfloat16 [24, 576, 768], P('ep', 'seq'), may hold values from -6 to 6
- routes: int32 [24, 576, 2], P('ep', 'seq'), may hold values from 0 to 31, all different within a row
- priority: int32 [24, 576], P('ep', 'seq'), may hold values from 0 to 431, as said below
- hires: int32 [8], P('ep'), may hold values from 0 to 3
- gain_one: float32 [768], replicated, may hold values from 0.1 to 1.9
- shift_one: float32 [768], replicated, may hold values from -1.8 to 1.8
- w_qkv: bfloat16 [768, 2304], replicated, may hold values from -0.21875 to 0.21875
- w_proj: bfloat16 [768, 768], replicated, may hold values from -6 to 6
- gain_two: float32 [768], replicated, may hold values from 0.1 to 1.9
- shift_two: float32 [768], replicated, may hold values from -1.8 to 1.8
- w_router: bfloat16 [768, 32], replicated, may hold values from -0.15917969 to 0.15917969
- expert_in: bfloat16 [98304, 768], P('ep'), may hold values from -0.21875 to 0.21875
- expert_out: bfloat16 [98304, 768], P('ep'), may hold values from -2.5 to 2.5
- cotangent: bfloat16 [24, 576, 768], P('ep', 'seq'), may hold values from -6 to 6
Outputs:
- output: bfloat16 [24, 576, 768], P('ep', 'seq')
- input_grad: bfloat16 [24, 576, 768], P('ep', 'seq')
- gain_one_grad: float32 [768], replicated
- shift_one_grad: float32 [768], replicated
- qkv_grad: float32 [768, 2304], replicated
- proj_grad: float32 [768, 768], replicated
- gain_two_grad: float32 [768], replicated
- shift_two_grad: float32 [768], replicated
- router_grad: float32 [768, 32], replicated
- expert_in_grad: float32 [98304, 768], P('ep')
- expert_out_grad: float32 [98304, 768], P('ep')
- rms_stats: float32 [3], replicated
Inputs may be any that keep to these rules, and one draw needn't show every extreme that they name: `priority`: within each device block of 3 images times 144 positions, the priorities are a permutation of 0 to 431.
All inputs are finite; a program needn't handle non-finite values.
Results may differ from a plain program's by a relative error of at most 0.015.
Values may be sent and summed in bfloat16 or wider, within the bound.
No kernel may reach another device: no remote copies, remote signals or barrier semaphores. Data moves between devices by JAX's collectives and lax.ppermute only.
A program may use at most 320 MiB of HBM per device.

v0:
```python
import jax
import jax.numpy as jnp
from jax import lax
from jax.sharding import PartitionSpec as P

HEADS = 12
EXPERTS = 32
TOP = 2
PATCHES = 576
SHORT = 196
norm_eps = 1e-06
neg_big = -1e30


def norm_forward(values, norm_gain, norm_bias):
    row_mean = jnp.mean(values, axis=-1, keepdims=True)
    centred = values - row_mean
    inv_root = lax.rsqrt(jnp.mean(centred * centred, axis=-1, keepdims=True) + norm_eps)
    normed = centred * inv_root
    return (normed * norm_gain + norm_bias, normed, inv_root)


def norm_backward(grad_out, normed, inv_root, norm_gain):
    gain_grad = jnp.sum(grad_out * normed, axis=0)
    bias_grad = jnp.sum(grad_out, axis=0)
    scaled = grad_out * norm_gain
    grad_in = inv_root * (
        scaled
        - jnp.mean(scaled, axis=-1, keepdims=True)
        - normed * jnp.mean(scaled * normed, axis=-1, keepdims=True)
    )
    return (grad_in, gain_grad, bias_grad)


def gelu_slope(values):
    return (
        0.5 * (1.0 + lax.erf(values * 0.7071067811865476))
        + values * jnp.exp(-0.5 * values * values) * 0.3989422804014327
    )


def routing(route_rows, priority_rows, row_valid, capacity):
    row_total = route_rows.shape[0]
    by_priority = (
        jnp.zeros((row_total,), jnp.int32)
        .at[priority_rows]
        .set(jnp.arange(row_total, dtype=jnp.int32))
    )
    ordered = jnp.concatenate([route_rows[by_priority, route_rank] for route_rank in range(TOP)])
    ordered_valid = jnp.concatenate([row_valid[by_priority]] * TOP)
    expert_hits = (
        ordered[:, None] == jnp.arange(EXPERTS, dtype=jnp.int32)[None, :]
    ) & ordered_valid[:, None]
    running = jnp.cumsum(expert_hits.astype(jnp.int32), axis=0)
    ordered_slot = jnp.sum(jnp.where(expert_hits, running, 0), axis=1) - 1
    pair_slot = ordered_slot.reshape(TOP, row_total)[:, priority_rows].T
    is_kept = (pair_slot >= 0) & (pair_slot < capacity)
    return jnp.where(is_kept, route_rows * capacity + pair_slot, EXPERTS * capacity)


def slot_sources(slot_dest, fill_value, capacity, divisor):
    flat_dest = slot_dest.reshape(-1)
    source_ids = jnp.arange(flat_dest.shape[0], dtype=jnp.int32) // divisor
    table_ids = (
        jnp.full((EXPERTS * capacity + 1,), fill_value, jnp.int32).at[flat_dest].set(source_ids)
    )
    return table_ids[: EXPERTS * capacity]


def fan_out(slot_table, ep_count, split_count, local_experts, capacity):
    feature_width = slot_table.shape[-1]
    grouped = slot_table.reshape(ep_count // split_count, 1, local_experts, capacity, feature_width)
    spread = jnp.broadcast_to(
        grouped, (ep_count // split_count, split_count, local_experts, capacity, feature_width)
    )
    return spread.reshape(ep_count, local_experts, capacity, feature_width)


def fan_in(arrived, split_count):
    ep_count, local_experts, capacity, feature_width = arrived.shape
    grouped = arrived.reshape(
        ep_count // split_count, split_count, local_experts, capacity, feature_width
    )
    return jnp.sum(grouped.astype(jnp.float32), axis=1).reshape(-1, feature_width)


def score_block(query_heads, key_heads, key_mask, score_scale):
    raw_scores = (
        jnp.einsum("ishd,ithd->ihst", query_heads, key_heads, preferred_element_type=jnp.float32)
        * score_scale
    )
    return jnp.where(key_mask[:, None, None, :], raw_scores, neg_big)


def per_device(
    tokens,
    routes,
    priority,
    hires,
    gain_one,
    shift_one,
    w_qkv,
    w_proj,
    gain_two,
    shift_two,
    w_router,
    expert_in,
    expert_out,
    cotangent,
):
    image_count, patch_rows, model_width = tokens.shape
    row_count = image_count * patch_rows
    seq_count = lax.axis_size("seq")
    ep_count = lax.axis_size("ep")
    full_patches = patch_rows * seq_count
    head_width = model_width // HEADS
    score_scale = head_width ** (-0.5)
    local_experts = max(1, EXPERTS // ep_count)
    split_count = max(1, ep_count // EXPERTS)
    local_hidden = expert_in.shape[0] // local_experts
    capacity = max(2, (105 * TOP * row_count + 100 * EXPERTS - 1) // (100 * EXPERTS))
    seq_place = lax.axis_index("seq")

    def send_slots(slot_table):
        outgoing = fan_out(slot_table, ep_count, split_count, local_experts, capacity)
        return lax.all_to_all(outgoing, "ep", split_axis=0, concat_axis=0, tiled=True)

    def return_slots(part_rows):
        returned = lax.all_to_all(part_rows, "ep", split_axis=0, concat_axis=0, tiled=True)
        return fan_in(returned, split_count)

    image_length = jnp.where(jnp.arange(image_count, dtype=jnp.int32) < hires[0], PATCHES, SHORT)
    key_mask = jnp.arange(full_patches, dtype=jnp.int32)[None, :] < image_length[:, None]
    own_mask = (seq_place * patch_rows + jnp.arange(patch_rows, dtype=jnp.int32))[
        None, :
    ] < image_length[:, None]
    row_valid = own_mask.reshape(row_count)
    valid_col = row_valid.astype(jnp.float32)[:, None]
    inputs = tokens.reshape(row_count, model_width).astype(jnp.float32)
    head_shape = (image_count, -1, HEADS, head_width)
    first_out, normed_one, inv_one = norm_forward(inputs, gain_one, shift_one)
    attn_in = first_out.astype(jnp.bfloat16)
    packed = jnp.dot(attn_in, w_qkv, preferred_element_type=jnp.float32).astype(jnp.bfloat16)
    query_rows = packed[:, :model_width].reshape(image_count, patch_rows, model_width)
    key_rows = packed[:, model_width : 2 * model_width].reshape(
        image_count, patch_rows, model_width
    )
    value_rows = packed[:, 2 * model_width :].reshape(image_count, patch_rows, model_width)
    query_heads = query_rows.reshape(head_shape)
    keys_all, values_all = (
        lax.all_gather(key_rows, "seq", axis=1, tiled=True),
        lax.all_gather(value_rows, "seq", axis=1, tiled=True),
    )
    scores = score_block(query_heads, keys_all.reshape(head_shape), key_mask, score_scale)
    row_max = jnp.max(scores, axis=-1, keepdims=True)
    exp_scores = jnp.exp(scores - row_max)
    row_total = jnp.sum(exp_scores, axis=-1, keepdims=True)
    probs = exp_scores / row_total
    log_total = row_max + jnp.log(row_total)
    attended = (
        jnp.einsum(
            "ihst,ithd->ishd",
            probs.astype(jnp.bfloat16),
            values_all.reshape(head_shape),
            preferred_element_type=jnp.float32,
        )
        .reshape(row_count, model_width)
        .astype(jnp.bfloat16)
    )
    attn_out = jnp.dot(attended, w_proj, preferred_element_type=jnp.float32)
    middle = inputs + attn_out
    second_out, normed_two, inv_two = norm_forward(middle, gain_two, shift_two)
    moe_in = second_out.astype(jnp.bfloat16)
    logits = jnp.dot(moe_in, w_router, preferred_element_type=jnp.float32)
    gate_probs = jax.nn.softmax(logits, axis=-1)
    route_rows = routes.reshape(row_count, TOP)
    slot_dest = routing(route_rows, priority.reshape(row_count), row_valid, capacity)
    token_src = slot_sources(slot_dest, row_count, capacity, TOP)
    pair_src = slot_sources(slot_dest, row_count * TOP, capacity, 1)
    padded_in = jnp.concatenate([moe_in, jnp.zeros((1, model_width), jnp.bfloat16)], axis=0)
    arrived = send_slots(padded_in[token_src])
    w_first = expert_in.reshape(local_experts, local_hidden, model_width)
    w_second = expert_out.reshape(local_experts, local_hidden, model_width)
    pre_act = jnp.einsum("secd,efd->secf", arrived, w_first, preferred_element_type=jnp.float32)
    hidden = jax.nn.gelu(pre_act, approximate=False).astype(jnp.bfloat16)
    partial_out = jnp.einsum(
        "secf,efd->secd", hidden, w_second, preferred_element_type=jnp.float32
    ).astype(jnp.bfloat16)
    value_table = return_slots(partial_out)
    padded_values = jnp.concatenate([value_table, jnp.zeros((1, model_width), jnp.float32)], axis=0)
    pair_values = padded_values[slot_dest.reshape(-1)].reshape(row_count, TOP, model_width)
    chosen = jnp.take_along_axis(gate_probs, route_rows, axis=1)
    moe_out = jnp.sum(chosen[:, :, None] * pair_values, axis=1)
    total = middle + moe_out
    output = (total * valid_col).astype(jnp.bfloat16).reshape(image_count, patch_rows, model_width)
    stat_terms = jnp.stack(
        [
            jnp.sum(valid_col * attn_out * attn_out),
            jnp.sum(valid_col * moe_out * moe_out),
            jnp.sum(valid_col * total * total),
            jnp.sum(row_valid.astype(jnp.float32)) * model_width,
        ]
    )
    grad_total = cotangent.reshape(row_count, model_width).astype(jnp.float32) * valid_col
    grad_gate = jnp.sum(grad_total[:, None, :] * pair_values, axis=2)
    grad_value = (
        (grad_total[:, None, :] * chosen[:, :, None])
        .astype(jnp.bfloat16)
        .reshape(row_count * TOP, model_width)
    )
    padded_grad = jnp.concatenate([grad_value, jnp.zeros((1, model_width), jnp.bfloat16)], axis=0)
    grad_sent = send_slots(padded_grad[pair_src])
    grad_hidden = jnp.einsum(
        "secd,efd->secf", grad_sent, w_second, preferred_element_type=jnp.float32
    )
    grad_pre = (grad_hidden * gelu_slope(pre_act)).astype(jnp.bfloat16)
    grad_second = jnp.einsum(
        "secf,secd->efd", hidden, grad_sent, preferred_element_type=jnp.float32
    ).reshape(-1, model_width)
    grad_first = jnp.einsum(
        "secf,secd->efd", grad_pre, arrived, preferred_element_type=jnp.float32
    ).reshape(-1, model_width)
    grad_part_in = jnp.einsum(
        "secf,efd->secd", grad_pre, w_first, preferred_element_type=jnp.float32
    ).astype(jnp.bfloat16)
    grad_in_table = return_slots(grad_part_in)
    padded_back = jnp.concatenate([grad_in_table, jnp.zeros((1, model_width), jnp.float32)], axis=0)
    grad_dispatch = jnp.sum(
        padded_back[slot_dest.reshape(-1)].reshape(row_count, TOP, model_width), axis=1
    )
    expert_ids = jnp.arange(EXPERTS, dtype=jnp.int32)
    grad_probs = jnp.sum(
        jnp.where(route_rows[:, :, None] == expert_ids[None, None, :], grad_gate[:, :, None], 0.0),
        axis=1,
    )
    grad_logits = (
        gate_probs * (grad_probs - jnp.sum(grad_probs * gate_probs, axis=-1, keepdims=True))
    ).astype(jnp.bfloat16)
    grad_router = jnp.einsum("rd,re->de", moe_in, grad_logits, preferred_element_type=jnp.float32)
    grad_moe_in = grad_dispatch + jnp.einsum(
        "re,de->rd", grad_logits, w_router, preferred_element_type=jnp.float32
    )
    grad_mid_norm, grad_gain_two, grad_shift_two = norm_backward(
        grad_moe_in, normed_two, inv_two, gain_two
    )
    grad_middle = grad_total + grad_mid_norm
    grad_attn = grad_middle.astype(jnp.bfloat16)
    grad_proj = jnp.einsum("rd,re->de", attended, grad_attn, preferred_element_type=jnp.float32)
    grad_attended = jnp.einsum(
        "re,de->rd", grad_attn, w_proj, preferred_element_type=jnp.float32
    ).astype(jnp.bfloat16)
    grad_heads = grad_attended.reshape(head_shape)
    keys_again, values_again = (
        lax.all_gather(key_rows, "seq", axis=1, tiled=True),
        lax.all_gather(value_rows, "seq", axis=1, tiled=True),
    )
    key_heads = keys_again.reshape(head_shape)
    value_heads = values_again.reshape(head_shape)
    probs_again = jnp.exp(score_block(query_heads, key_heads, key_mask, score_scale) - log_total)
    grad_probs_att = jnp.einsum(
        "ishd,ithd->ihst", grad_heads, value_heads, preferred_element_type=jnp.float32
    )
    delta = jnp.sum(grad_probs_att * probs_again, axis=-1, keepdims=True)
    grad_scores = (probs_again * (grad_probs_att - delta)).astype(jnp.bfloat16)
    grad_queries = (
        jnp.einsum("ihst,ithd->ishd", grad_scores, key_heads, preferred_element_type=jnp.float32)
        * score_scale
    )
    grad_keys_full = (
        jnp.einsum("ihst,ishd->ithd", grad_scores, query_heads, preferred_element_type=jnp.float32)
        * score_scale
    )
    grad_values_full = jnp.einsum(
        "ihst,ishd->ithd",
        probs_again.astype(jnp.bfloat16),
        grad_heads,
        preferred_element_type=jnp.float32,
    )
    grad_keys, grad_values = (
        lax.psum_scatter(
            grad_keys_full.reshape(image_count, full_patches, model_width),
            "seq",
            scatter_dimension=1,
            tiled=True,
        ),
        lax.psum_scatter(
            grad_values_full.reshape(image_count, full_patches, model_width),
            "seq",
            scatter_dimension=1,
            tiled=True,
        ),
    )
    grad_packed = jnp.concatenate(
        [
            grad_queries.reshape(row_count, model_width),
            grad_keys.reshape(row_count, model_width),
            grad_values.reshape(row_count, model_width),
        ],
        axis=1,
    ).astype(jnp.bfloat16)
    grad_qkv = jnp.einsum("rd,re->de", attn_in, grad_packed, preferred_element_type=jnp.float32)
    grad_attn_in = jnp.einsum("re,de->rd", grad_packed, w_qkv, preferred_element_type=jnp.float32)
    grad_in_norm, grad_gain_one, grad_shift_one = norm_backward(
        grad_attn_in, normed_one, inv_one, gain_one
    )
    input_grad = (
        (grad_middle + grad_in_norm)
        .astype(jnp.bfloat16)
        .reshape(image_count, patch_rows, model_width)
    )
    summed = lax.psum(
        (
            grad_qkv,
            grad_proj,
            grad_router,
            grad_gain_one,
            grad_shift_one,
            grad_gain_two,
            grad_shift_two,
            stat_terms,
        ),
        ("seq", "ep"),
    )
    expert_grads = (
        lax.psum(grad_first.astype(jnp.bfloat16), "seq").astype(jnp.float32),
        lax.psum(grad_second.astype(jnp.bfloat16), "seq").astype(jnp.float32),
    )
    rms_stats = jnp.sqrt(summed[7][:3] / summed[7][3])
    return (
        output,
        input_grad,
        summed[3],
        summed[4],
        summed[0],
        summed[1],
        summed[5],
        summed[6],
        summed[2],
        expert_grads[0],
        expert_grads[1],
        rms_stats,
    )


def solution(mesh):
    in_specs = (
        P("ep", "seq", None),
        P("ep", "seq", None),
        P("ep", "seq"),
        P("ep"),
        P(),
        P(),
        P(),
        P(),
        P(),
        P(),
        P(),
        P("ep", None),
        P("ep", None),
        P("ep", "seq", None),
    )
    out_specs = (
        P("ep", "seq", None),
        P("ep", "seq", None),
        P(),
        P(),
        P(),
        P(),
        P(),
        P(),
        P(),
        P("ep", None),
        P("ep", None),
        P(),
    )
    return jax.shard_map(
        per_device, mesh=mesh, in_specs=in_specs, out_specs=out_specs, check_vma=False
    )
```

profile of v0, /device:TPU:0, one launch (start us, length us, event | category | flops | bytes accessed | tf_op | source)
XLA Modules:
  0.0 1413.0 jit_solution(5902060563627623308)
XLA Ops:
  15.6 3.3 reshape_reshape.9
  18.9 3.8 copy.111
  28.5 6.5 gather_fusion
  35.0 7.7 gather_fusion.1
  44.1 4.0 gather_fusion.2
  50.4 4.8 reduce-window.6
  65.3 5.5 scatter_custom_fusion.1
  71.5 5.4 copy.110
  76.9 5.0 fusion.69
  81.9 5.0 copy-done.1
  86.9 3.8 fusion.23
  90.7 9.3 all-gather.3.cloned.1.call-done
  100.0 5.3 copy.109
  105.3 8.2 fusion.37
  113.5 4.0 copy.112
  117.5 3.5 convert_element_type.128
  121.0 3.5 fusion.67
  127.9 6.7 gather_fusion.4
  137.0 3.6 copy.119
  140.7 5.1 all-to-all-start
  156.2 4.6 mul.269
  160.8 5.4 scatter_custom_fusion.2
  169.5 12.0 gather_fusion.8
  184.7 7.0 gather_fusion.6
  194.2 3.7 copy.124
  197.8 5.3 all-to-all-start.2
  203.2 35.2 %fusion.2 = (bf16[8,4,29,3072]{3,2,0,1:T(8,128)(2,1)S(1)}, f32[4,8,29,3072]{3,2,1,0:T(8,128)}) fusion(bf16[4,3072,768,1]{2,1,3,0:T(8,128)(2,1)} %bitcast.184, bf16[8,4,29,768]{3,1,2,0:T(4,128)(2,1)} %all-to-all-done), kind=kOutput, calls=%fused_computation.24 | convolution fusion | flops 4564156416 | bytes 37404672 | tf_op jit(solution)/shard_map/secd,efd->secf/dot_general | solution.py:184
  238.3 11.5 fusion.30
  252.0 5.6 all-to-all-start.1
  257.6 13.6 fusion.8
  271.3 11.5 fusion.31
  285.0 7.3 all-to-all-done.1
  292.3 4.3 all-to-all-start.3
  310.3 6.7 gather_fusion.5
  317.0 4.4 reshape.414
  321.4 7.5 multiply_reduce_fusion.1
  342.1 6.7 gather_fusion.7
  348.8 4.6 reshape.418
  353.4 6.0 reduce_sum.241
  359.5 5.4 fusion.41
  368.1 3.3 reshape.419
  371.4 3.8 copy.130
  375.2 14.9 %multiply_reduce_fusion = (f32[3,12,144]{2,1,0:T(8,128)S(1)}, f32[3,12,144,576]{3,2,1,0:T(8,128)}) fusion(f32[3,12,144,576]{3,2,1,0:T(8,128)} %copy-done.1, f32[3,12,144]{2,1,0:T(8,128)} %log_add_fusion, bf16[3,144,12,64]{1,3,2,0:T(8,128)(2,1)} %copy.130, bf16[3,576,12,64]{1,3,2,0:T(8,128)(2,1)} %bitcast.170), kind=kOutput, calls=%fused_computation.17 | convolution fusion | flops 391158720 | bytes 27247104 | tf_op jit(solution)/shard_map/ishd,ithd->ihst/dot_general | solution.py:260
  390.1 9.9 multiply_convert_fusion
  400.1 4.2 broadcast_multiply_fusion
  404.7 7.5 copy.133
  412.2 9.9 fusion.25
  422.1 7.5 copy.135
  429.7 12.3 bitcast_convert_fusion
  442.0 12.1 bitcast_convert_fusion.1
  454.2 8.4 fusion.38
  462.6 4.2 copy.131
  466.9 3.5 reshape.420
  472.4 3.7 fusion.44
  478.4 61.2 %reduce-scatter.5.cloned.1.call-done = f32[3,144,768]{2,1,0:T(8,128)} async-done(((f32[3,576,768]{2,1,0:T(8,128)}), f32[3,144,768]{2,1,0:T(8,128)}) %reduce-scatter.5.cloned.1.call-update) | async-done | bytes 1327120 | tf_op jit(solution)/shard_map/reduce_scatter | solution.py:286
  541.8 6.5 fusion.42
  551.5 5.5 multiply_reduce_fusion.4
  557.0 40.4 %all-reduce.7 = (f32[768]{0:T(1024)}, f32[768]{0:T(1024)}, f32[768]{0:T(1024)}, f32[768]{0:T(1024)}, f32[4]{0:T(128)}) all-reduce(f32[768]{0:T(1024)} %get-tuple-element.17, f32[768]{0:T(1024)} %get-tuple-element.26, f32[768]{0:T(1024)S(1)} %copy-done.36, f32[768]{0:T(1024)S(1)} %copy-done.37, ...), channel_id=1, replica_groups=mesh['seq'=4,'ep'=8] {'seq','ep'}, use_global_device_ids=true, to_apply=%region_27.28 | all-reduce | flops 3076 | bytes 24608 | tf_op jit(solution)/shard_map/psum | solution.py:311
  605.1 588.1 %all-reduce.15.cloned.1.call-done = (bf16[12288,768]{1,0:T(8,128)(2,1)}, bf16[12288,768]{1,0:T(8,128)(2,1)}) async-done(((bf16[12288,768]{1,0:T(8,128)(2,1)}, bf16[12288,768]{1,0:T(8,128)(2,1)}), (bf16[12288,768]{1,0:T(8,128)(2,1)}, bf16[12288,768]{1,0:T(8,128)(2,1)})) %all-reduce.15.cloned.1.call-update) | async-done | bytes 37748752 | tf_op jit(solution)/shard_map/psum | solution.py:325
  1193.2 21.1 %convert_element_type.149 = f32[12288,768]{1,0:T(8,128)} convert(bf16[12288,768]{1,0:T(8,128)(2,1)} %get-tuple-element.36) | non-fusion elementwise | flops 9437184 | bytes 56623104 | tf_op jit(solution)/shard_map/convert_element_type | solution.py:325
  1214.2 4.6 copy-done.6
  1218.9 12.9 convert_element_type.152
  1231.8 165.5 %all-reduce.13.cloned.1.call-done = (f32[768,2304]{1,0:T(8,128)}, f32[768,768]{1,0:T(8,128)}, f32[768,32]{0,1:T(8,128)}) async-done(((f32[768,2304]{1,0:T(8,128)}, f32[768,768]{1,0:T(8,128)}, f32[768,32]{0,1:T(8,128)}), (f32[768,2304]{1,0:T(8,128)}, f32[768,768]{1,0:T(8,128)}, f32[768,32]{0,1:T(8,128)})) %all-reduce.13.cloned.1.call-update) | async-done | bytes 9535504 | tf_op jit(solution)/shard_map/psum | solution.py:311
  1397.3 6.6 copy.162
  (205 shorter events, 106.9 us)
Async XLA Ops:
  7.2 4.6 copy-start
  7.2 64.3 %all-gather.5.cloned.1.call-start = ((), (), s32[]{:S(2)}) async-start(), calls=%async_computation.7 | async-start | bytes 3317760 | tf_op jit(solution)/shard_map/all_gather | solution.py:151
  10.2 3.3 copy-start.32
  10.3 3.2 copy-start.34
  11.8 1.8 copy-start.12
  14.9 85.1 %all-gather.3.cloned.1.call-start = ((), (), s32[]{:S(2)}) async-start(), calls=%async_computation.6 | async-start | bytes 3317760 | tf_op jit(solution)/shard_map/all_gather | solution.py:152
  14.9 8.9 copy-start.31
  15.6 9.1 copy-start.44
  24.8 0.6 copy-start.41
  49.0 6.3 copy-start.43
  65.3 5.5 copy-start.39
  81.9 5.0 copy-start.1
  81.9 5.0 copy-start.17
  121.0 4.5 copy-start.23
  121.0 4.5 copy-start.42
  124.5 1.1 copy-start.3
  124.5 1.3 copy-start.19
  125.6 0.6 copy-start.27
  126.1 0.9 copy-start.8
  140.7 57.1 %all-to-all-start = ((bf16[8,4,29,768]{3,1,2,0:T(4,128)(2,1)}), bf16[8,4,29,768]{3,1,2,0:T(4,128)(2,1)}, u32[]{:S(2)}, u32[]{:S(2)}) async-start(bf16[8,4,29,768]{3,1,2,0:T(4,128)(2,1)} %copy.119), calls=%async_computation | async-start | bytes 2850816 | tf_op jit(solution)/shard_map/all_to_all | solution.py:126
  146.5 9.8 copy-start.25
  152.7 1.1 copy-start.7
  167.7 0.6 copy-start.15
  167.7 0.6 copy-start.21
  168.3 0.6 copy-start.29
  169.5 12.0 copy-start.38
  197.8 54.2 %all-to-all-start.2 = ((bf16[8,4,29,768]{3,1,2,0:T(4,128)(2,1)}), bf16[8,4,29,768]{3,1,2,0:T(4,128)(2,1)}, u32[]{:S(2)}, u32[]{:S(2)}) async-start(bf16[8,4,29,768]{3,1,2,0:T(4,128)(2,1)} %copy.124), calls=%async_computation.2 | async-start | bytes 2850816 | tf_op jit(solution)/shard_map/all_to_all | solution.py:126
  238.3 11.5 copy-start.46
  252.0 40.3 %all-to-all-start.1 = ((bf16[8,4,29,768]{3,1,2,0:T(4,128)(2,1)}), bf16[8,4,29,768]{3,1,2,0:T(4,128)(2,1)}, u32[]{:S(2)}, u32[]{:S(2)}) async-start(bf16[8,4,29,768]{3,1,2,0:T(4,128)(2,1)} %copy.121), calls=%async_computation.1 | async-start | bytes 2850816 | tf_op jit(solution)/shard_map/all_to_all | solution.py:129
  271.3 11.5 copy-start.45
  282.8 15.0 %copy-start.40 = (s32[864]{0:T(1024)S(1)}, s32[864]{0:T(1024)}, u32[]{:S(2)}) copy-start(s32[864]{0:T(1024)} %copy-done.39) | copy-start | bytes 10372
  292.3 41.4 %all-to-all-start.3 = ((bf16[8,4,29,768]{3,1,2,0:T(4,128)(2,1)}), bf16[8,4,29,768]{3,1,2,0:T(4,128)(2,1)}, u32[]{:S(2)}, u32[]{:S(2)}) async-start(bf16[8,4,29,768]{3,1,2,0:T(4,128)(2,1)} %copy.126), calls=%async_computation.3 | async-start | bytes 2850816 | tf_op jit(solution)/shard_map/all_to_all | solution.py:129
  296.6 179.5 %reduce-scatter.3.cloned.1.call-start = ((), (), s32[]{:S(2)}) async-start(), calls=%async_computation.8 | async-start | bytes 6635520 | tf_op jit(solution)/shard_map/reduce_scatter | solution.py:280
  321.4 9.9 copy-start.22
  321.4 9.9 copy-start.30
  353.4 6.0 copy-start.20
  353.4 6.0 copy-start.24
  353.4 6.0 copy-start.26
  353.4 6.0 copy-start.28
  359.4 5.5 copy-start.4
  359.4 5.4 copy-start.11
  364.9 1.7 copy-start.10
  365.4 1.1 copy-start.5
  375.2 14.9 %copy-start.16 = (f32[3,12,144]{2,1,0:T(8,128)S(1)}, f32[3,12,144]{2,1,0:T(8,128)}, u32[]{:S(2)}) copy-start(f32[3,12,144]{2,1,0:T(8,128)} %log_add_fusion) | copy-start | bytes 62212
  390.1 9.9 copy-start.9
  400.1 4.6 copy-start.2
  412.1 127.4 %reduce-scatter.5.cloned.1.call-start = ((), (), s32[]{:S(2)}) async-start(), calls=%async_computation.9 | async-start | bytes 6635520 | tf_op jit(solution)/shard_map/reduce_scatter | solution.py:286
  429.7 763.5 %all-reduce.15.cloned.1.call-start = ((), (), s32[]{:S(2)}) async-start(), calls=%async_computation.11 | async-start | bytes 75497472 | tf_op jit(solution)/shard_map/psum | solution.py:325
  454.2 943.1 %all-reduce.13.cloned.1.call-start = ((), (), s32[]{:S(2)}) async-start(), calls=%async_computation.10 | async-start | bytes 19070976 | tf_op jit(solution)/shard_map/psum | solution.py:311
  540.9 0.8 copy-start.13
  548.3 3.2 copy-start.33
  548.3 3.2 copy-start.35
  551.5 5.5 copy-start.36
  551.5 5.5 copy-start.37
  1193.2 25.7 %copy-start.6 = (bf16[12288,768]{1,0:T(8,128)(2,1)S(1)}, bf16[12288,768]{1,0:T(8,128)(2,1)}, u32[]{:S(2)}) copy-start(bf16[12288,768]{1,0:T(8,128)(2,1)} %get-tuple-element.37) | copy-start | bytes 56623108
  1397.3 6.6 copy-start.14
  1403.9 1.4 copy-start.18
Sparse Core Ops, SparseCore 0:
  15.0 42.6 all-gather.4
  60.1 39.9 all-gather.2
  412.3 62.3 reduce-scatter.2
  477.5 61.9 reduce-scatter.4
  543.7 649.4 all-reduce.14
  1201.5 195.7 all-reduce.12
where the time goes:
time: 1420 us; the launch traced here: 1410 us
  waiting for transfers between devices  832 us (59%)
  local copies, waits for them, and re-layouts  215 us (15%)
  matrix products  178 us (13%)
  other arithmetic  110 us (8%)
  blocking collectives  40.4 us (3%)
  starting transfers between devices  20.5 us (1%)
  between operations  16.3 us (1%)
    psum x1, waiting for transfers between devices, per_device(): lax.psum(grad_first.astype(jnp.bfloat16), 'seq').astype(jnp.float32)  588 us
    psum x1, waiting for transfers between devices, per_device(): lax.psum((grad_qkv, grad_proj, grad_router, grad_gain_one, grad_shift_one...  165 us
    reduce_scatter x1, waiting for transfers between devices, per_device(): lax.psum_scatter(grad_values_full.reshape(image_count, full_patches, mode...  61.2 us
    psum x1, blocking collectives, per_device(): lax.psum((grad_qkv, grad_proj, grad_router, grad_gain_one, grad_shift_one...  40.4 us
    dot_general x1, matrix products, per_device(): jnp.einsum('secd,efd->secf', arrived, w_first, preferred_element_type=jnp...  35.2 us
  transfers between devices with their start and end apart: 10, of which 5 were waited for; matrix products, arithmetic and copies ran while one was open for 25% of the time, Pallas kernels for 0%

commit v1 on v0

--- a/solution.py
+++ b/solution.py
@@ -322,7 +322,7 @@
         ("seq", "ep"),
     )
     expert_grads = (
-        lax.psum(grad_first.astype(jnp.bfloat16), "seq").astype(jnp.float32),
+        jnp.sum(lax.all_gather(grad_first.astype(jnp.bfloat16), "seq"), axis=0).astype(jnp.float32),
         lax.psum(grad_second.astype(jnp.bfloat16), "seq").astype(jnp.float32),
     )
     rms_stats = jnp.sqrt(summed[7][:3] / summed[7][3])

time: 1420 us -> 1760 us (1.24)
  waiting for transfers between devices: 832 us -> 1130 us
  other arithmetic: 110 us -> 158 us
    all_gather x0 -> x1, waiting for transfers between devices: none -> 627 us  [per_device(): lax.all_gather(grad_first.astype(jnp.bfloat16), 'seq')]
    psum x1, waiting for transfers between devices: 588 us -> 281 us  [per_device(): lax.psum(grad_second.astype(jnp.bfloat16), 'seq').astype(jnp.float32)]
    reduce_sum x0 -> x1, other arithmetic: none -> 36.7 us  [per_device(): jnp.sum(lax.all_gather(grad_first.astype(jnp.bfloat16), 'seq'), axis=0)]
    psum x1, waiting for transfers between devices: 165 us -> 144 us  [per_device(): lax.psum((grad_qkv, grad_proj, grad_router, grad_gain_one, grad_shift_one...]
  transfers between devices with their start and end apart: 10 -> 11, of which waited for: 5 -> 6; matrix products, arithmetic and copies ran while one was open for 25% -> 23% of each run, Pallas kernels for 0% -> 0%
where the time goes in v1:
time: 1760 us
  waiting for transfers between devices  1130 us (64%)
  local copies, waits for them, and re-layouts  210 us (12%)
  matrix products  178 us (10%)
  other arithmetic  158 us (9%)
  blocking collectives  40.7 us (2%)
  starting transfers between devices  20.6 us (1%)
    all_gather x1, waiting for transfers between devices, per_device(): lax.all_gather(grad_first.astype(jnp.bfloat16), 'seq')  627 us
    psum x1, waiting for transfers between devices, per_device(): lax.psum(grad_second.astype(jnp.bfloat16), 'seq').astype(jnp.float32)  281 us
    psum x1, waiting for transfers between devices, per_device(): lax.psum((grad_qkv, grad_proj, grad_router, grad_gain_one, grad_shift_one...  144 us
    reduce_scatter x1, waiting for transfers between devices, per_device(): lax.psum_scatter(grad_values_full.reshape(image_count, full_patches, mode...  61.1 us
    psum x1, blocking collectives, per_device(): lax.psum((grad_qkv, grad_proj, grad_router, grad_gain_one, grad_shift_one...  40.7 us
    reduce_sum x1, other arithmetic, per_device(): jnp.sum(lax.all_gather(grad_first.astype(jnp.bfloat16), 'seq'), axis=0)  36.7 us
  transfers between devices with their start and end apart: 11, of which 6 were waited for; matrix products, arithmetic and copies ran while one was open for 23% of the time, Pallas kernels for 0%

profile of v1, /device:TPU:0, one launch (start us, length us, event | category | flops | bytes accessed | tf_op | source)
XLA Modules:
  0.0 1755.6 jit_solution(6469078707572773108)
XLA Ops:
  15.6 3.3 reshape_reshape.9
  18.9 3.8 copy.111
  28.5 6.5 gather_fusion
  35.1 7.7 gather_fusion.1
  44.2 4.0 gather_fusion.2
  50.5 4.8 reduce-window.6
  65.3 5.5 scatter_custom_fusion.1
  71.6 5.4 copy.110
  77.0 5.0 fusion.69
  82.0 5.0 copy-done.1
  86.9 3.8 fusion.23
  90.8 9.2 all-gather.4.cloned.1.call-done
  100.0 5.3 copy.109
  105.3 8.2 fusion.37
  113.5 4.0 copy.112
  117.5 3.5 convert_element_type.137
  121.0 3.5 fusion.67
  127.9 6.7 gather_fusion.4
  137.0 3.6 copy.119
  140.7 5.1 all-to-all-start
  156.3 4.6 mul.269
  160.9 5.4 scatter_custom_fusion.2
  169.6 12.0 gather_fusion.8
  184.8 7.0 gather_fusion.6
  194.2 3.6 copy.124
  197.9 5.3 all-to-all-start.2
  203.2 35.2 %fusion.2 = (bf16[8,4,29,3072]{3,2,0,1:T(8,128)(2,1)S(1)}, f32[4,8,29,3072]{3,2,1,0:T(8,128)}) fusion(bf16[4,3072,768,1]{2,1,3,0:T(8,128)(2,1)} %bitcast.184, bf16[8,4,29,768]{3,1,2,0:T(4,128)(2,1)} %all-to-all-done), kind=kOutput, calls=%fused_computation.24 | convolution fusion | flops 4564156416 | bytes 37404672 | tf_op jit(solution)/shard_map/secd,efd->secf/dot_general | solution.py:184
  238.4 11.5 fusion.30
  252.1 5.6 all-to-all-start.1
  257.7 13.6 fusion.8
  271.3 11.5 fusion.31
  285.0 7.3 all-to-all-done.1
  292.4 4.3 all-to-all-start.3
  310.4 6.7 gather_fusion.5
  317.0 4.4 reshape.424
  321.5 7.5 multiply_reduce_fusion.1
  342.2 6.7 gather_fusion.7
  348.9 4.6 reshape.428
  353.5 6.0 reduce_sum.253
  359.5 5.4 fusion.41
  371.4 3.8 copy.130
  375.2 14.9 multiply_reduce_fusion
  390.2 9.9 multiply_convert_fusion
  400.1 4.3 broadcast_multiply_fusion
  404.7 7.5 copy.133
  412.3 9.9 fusion.25
  422.2 7.5 copy.135
  429.8 12.3 bitcast_convert_fusion
  442.1 12.1 bitcast_convert_fusion.1
  454.4 8.5 fusion.38
  462.8 4.2 copy.131
  467.0 3.5 reshape.430
  472.6 3.7 fusion.44
  478.5 61.1 %reduce-scatter.5.cloned.1.call-done = f32[3,144,768]{2,1,0:T(8,128)} async-done(((f32[3,576,768]{2,1,0:T(8,128)}), f32[3,144,768]{2,1,0:T(8,128)}) %reduce-scatter.5.cloned.1.call-update) | async-done | bytes 1327120 | tf_op jit(solution)/shard_map/reduce_scatter | solution.py:286
  541.8 6.5 fusion.42
  551.5 5.5 multiply_reduce_fusion.4
  557.0 40.7 %all-reduce.7 = (f32[768]{0:T(1024)}, f32[768]{0:T(1024)}, f32[768]{0:T(1024)}, f32[768]{0:T(1024)}, f32[4]{0:T(128)}) all-reduce(f32[768]{0:T(1024)} %get-tuple-element.17, f32[768]{0:T(1024)} %get-tuple-element.26, f32[768]{0:T(1024)S(1)} %copy-done.35, f32[768]{0:T(1024)S(1)} %copy-done.36, ...), channel_id=1, replica_groups=mesh['seq'=4,'ep'=8] {'seq','ep'}, use_global_device_ids=true, to_apply=%region_27.28 | all-reduce | flops 3076 | bytes 24608 | tf_op jit(solution)/shard_map/psum | solution.py:311
  605.3 281.5 %all-reduce.12.cloned.1.call-done = bf16[12288,768]{1,0:T(8,128)(2,1)} async-done(((bf16[12288,768]{1,0:T(8,128)(2,1)}), bf16[12288,768]{1,0:T(8,128)(2,1)}) %all-reduce.12.cloned.1.call-update) | async-done | bytes 18874384 | tf_op jit(solution)/shard_map/psum | solution.py:326
  886.7 24.0 %convert_element_type.161 = f32[12288,768]{1,0:T(8,128)} convert(bf16[12288,768]{1,0:T(8,128)(2,1)} %all-reduce.12.cloned.1.call-done) | non-fusion elementwise | flops 9437184 | bytes 56623104 | tf_op jit(solution)/shard_map/convert_element_type | solution.py:326
  910.7 627.0 %all-gather.8.cloned.1.call-done = bf16[4,12288,768]{2,1,0:T(8,128)(2,1)} async-done(((bf16[1,12288,768]{2,1,0:T(8,128)(2,1)}), bf16[4,12288,768]{2,1,0:T(8,128)(2,1)}) %all-gather.8.cloned.1.call-update) | async-done | bytes 75497488 | tf_op jit(solution)/shard_map/all_gather | solution.py:325
  1537.7 36.7 %reduce_sum.266 = bf16[12288,768]{1,0:T(8,128)(2,1)} reduce(bf16[4,12288,768]{2,1,0:T(8,128)(2,1)} %all-gather.8.cloned.1.call-done, bf16[]{:T(256)} %constant.69.clone.1), dimensions={0}, to_apply=%region_37.38 | reduce | flops 28311552 | bytes 94371840 | tf_op jit(solution)/shard_map/reduce_sum | solution.py:325
  1574.4 21.0 %convert_element_type.158 = f32[12288,768]{1,0:T(8,128)} convert(bf16[12288,768]{1,0:T(8,128)(2,1)} %reduce_sum.266) | non-fusion elementwise | flops 9437184 | bytes 56623104 | tf_op jit(solution)/shard_map/convert_element_type | solution.py:325
  1595.4 144.2 %all-reduce.14.cloned.1.call-done = (f32[768,2304]{1,0:T(8,128)}, f32[768,768]{1,0:T(8,128)}, f32[768,32]{0,1:T(8,128)}) async-done(((f32[768,2304]{1,0:T(8,128)}, f32[768,768]{1,0:T(8,128)}, f32[768,32]{0,1:T(8,128)}), (f32[768,2304]{1,0:T(8,128)}, f32[768,768]{1,0:T(8,128)}, f32[768,32]{0,1:T(8,128)})) %all-reduce.14.cloned.1.call-update) | async-done | bytes 9535504 | tf_op jit(solution)/shard_map/psum | solution.py:311
  1739.7 6.6 copy.161
  (207 shorter events, 110.0 us)
Async XLA Ops:
  7.2 4.6 copy-start
  7.2 64.4 %all-gather.6.cloned.1.call-start = ((), (), s32[]{:S(2)}) async-start(), calls=%async_computation.7 | async-start | bytes 3317760 | tf_op jit(solution)/shard_map/all_gather | solution.py:151
  10.2 3.3 copy-start.31
  10.3 3.2 copy-start.33
  11.8 1.8 copy-start.11
  14.9 85.1 %all-gather.4.cloned.1.call-start = ((), (), s32[]{:S(2)}) async-start(), calls=%async_computation.6 | async-start | bytes 3317760 | tf_op jit(solution)/shard_map/all_gather | solution.py:152
  14.9 8.9 copy-start.30
  15.6 9.1 copy-start.43
  24.8 0.6 copy-start.40
  49.0 6.3 copy-start.42
  65.3 5.5 copy-start.38
  81.9 5.0 copy-start.1
  81.9 5.0 copy-start.16
  121.0 4.5 copy-start.22
  121.0 4.5 copy-start.41
  124.5 1.1 copy-start.3
  124.5 1.3 copy-start.18
  125.6 0.6 copy-start.26
  126.1 0.8 copy-start.7
  140.7 57.2 %all-to-all-start = ((bf16[8,4,29,768]{3,1,2,0:T(4,128)(2,1)}), bf16[8,4,29,768]{3,1,2,0:T(4,128)(2,1)}, u32[]{:S(2)}, u32[]{:S(2)}) async-start(bf16[8,4,29,768]{3,1,2,0:T(4,128)(2,1)} %copy.119), calls=%async_computation | async-start | bytes 2850816 | tf_op jit(solution)/shard_map/all_to_all | solution.py:126
  146.5 9.8 copy-start.24
  152.8 1.1 copy-start.6
  167.7 0.6 copy-start.14
  167.7 0.6 copy-start.20
  168.4 0.6 copy-start.28
  169.6 12.0 copy-start.37
  197.9 54.2 %all-to-all-start.2 = ((bf16[8,4,29,768]{3,1,2,0:T(4,128)(2,1)}), bf16[8,4,29,768]{3,1,2,0:T(4,128)(2,1)}, u32[]{:S(2)}, u32[]{:S(2)}) async-start(bf16[8,4,29,768]{3,1,2,0:T(4,128)(2,1)} %copy.124), calls=%async_computation.2 | async-start | bytes 2850816 | tf_op jit(solution)/shard_map/all_to_all | solution.py:126
  238.4 11.5 copy-start.45
  252.1 40.3 %all-to-all-start.1 = ((bf16[8,4,29,768]{3,1,2,0:T(4,128)(2,1)}), bf16[8,4,29,768]{3,1,2,0:T(4,128)(2,1)}, u32[]{:S(2)}, u32[]{:S(2)}) async-start(bf16[8,4,29,768]{3,1,2,0:T(4,128)(2,1)} %copy.121), calls=%async_computation.1 | async-start | bytes 2850816 | tf_op jit(solution)/shard_map/all_to_all | solution.py:129
  271.3 11.5 copy-start.44
  282.8 15.0 copy-start.39
  292.4 41.3 %all-to-all-start.3 = ((bf16[8,4,29,768]{3,1,2,0:T(4,128)(2,1)}), bf16[8,4,29,768]{3,1,2,0:T(4,128)(2,1)}, u32[]{:S(2)}, u32[]{:S(2)}) async-start(bf16[8,4,29,768]{3,1,2,0:T(4,128)(2,1)} %copy.126), calls=%async_computation.3 | async-start | bytes 2850816 | tf_op jit(solution)/shard_map/all_to_all | solution.py:129
  296.7 179.6 %reduce-scatter.3.cloned.1.call-start = ((), (), s32[]{:S(2)}) async-start(), calls=%async_computation.8 | async-start | bytes 6635520 | tf_op jit(solution)/shard_map/reduce_scatter | solution.py:280
  321.5 9.9 copy-start.21
  321.5 9.9 copy-start.29
  353.5 6.0 copy-start.19
  353.5 6.0 copy-start.23
  353.5 6.0 copy-start.25
  353.5 6.0 copy-start.27
  359.5 5.5 copy-start.4
  359.5 5.4 copy-start.10
  364.9 1.7 copy-start.9
  365.5 1.1 copy-start.5
  375.2 14.9 copy-start.15
  390.2 9.9 copy-start.8
  400.1 4.6 copy-start.2
  412.2 127.4 %reduce-scatter.5.cloned.1.call-start = ((), (), s32[]{:S(2)}) async-start(), calls=%async_computation.9 | async-start | bytes 6635520 | tf_op jit(solution)/shard_map/reduce_scatter | solution.py:286
  429.7 457.0 %all-reduce.12.cloned.1.call-start = ((), (), s32[]{:S(2)}) async-start(), calls=%async_computation.11 | async-start | bytes 37748736 | tf_op jit(solution)/shard_map/psum | solution.py:326
  442.1 1095.6 %all-gather.8.cloned.1.call-start = ((), (), s32[]{:S(2)}) async-start(), calls=%async_computation.10 | async-start | bytes 94371840 | tf_op jit(solution)/shard_map/all_gather | solution.py:325
  454.3 1285.3 %all-reduce.14.cloned.1.call-start = ((), (), s32[]{:S(2)}) async-start(), calls=%async_computation.12 | async-start | bytes 19070976 | tf_op jit(solution)/shard_map/psum | solution.py:311
  541.0 0.8 copy-start.12
  548.3 3.2 copy-start.32
  548.3 3.2 copy-start.34
  551.5 5.5 copy-start.35
  551.5 5.5 copy-start.36
  1739.7 6.6 copy-start.13
  1746.2 1.4 copy-start.17
Sparse Core Ops, SparseCore 0:
  15.0 42.6 all-gather.5
  60.1 39.9 all-gather.3
  412.3 62.3 reduce-scatter.2
  477.5 61.9 reduce-scatter.4
  543.5 343.1 all-reduce.11
  889.2 648.4 all-gather.7
  1546.2 193.4 all-reduce.13
